TPU v7x, 256 devices: a whole 4x4x8 slice. The times are simulated.
256 devices in a mesh: seq: 32 (over z, y), tp: 8 (over x, core).
Axes of the slice: x: 4, y: 4, z: 8, core: 2. Of those that a mesh axis runs over, the one named last changes fastest.
Arguments:
- query_raw: bfloat16 [16384, 4096], P('seq', 'tp'), may hold values from -6 to 6
- key_raw: bfloat16 [16384, 4096], P('seq', 'tp'), may hold values from -6 to 6
- value_raw: bfloat16 [16384, 4096], P('seq', 'tp'), may hold values from -6 to 6
- conv_taps: float32 [3, 4, 4096], P(None, None, 'tp'), may hold values from -3 to 3
- layout_boxes: int32 [4, 16384], P(None, 'seq'), may hold values from 0 to 1023
- box_tables: bfloat16 [2, 1024, 4096], P(None, None, 'tp'), may hold values from -4 to 4
- log_decay: float32 [32, 16384], P('tp', 'seq'), may hold values from -1 to 0, as said below
- norm_gain: float32 [4096], P('tp'), may hold values from 0.25 to 1.75
- out_weight: bfloat16 [4096, 4096], P('tp', 'seq'), may hold values from -0.09375 to 0.09375
- grad_output: bfloat16 [16384, 4096], P('seq', 'tp'), may hold values from -6 to 6
Outputs:
- layer_out: bfloat16 [16384, 4096], P('seq', 'tp')
- grad_query: bfloat16 [16384, 4096], P('seq', 'tp')
- grad_key: bfloat16 [16384, 4096], P('seq', 'tp')
- grad_value: bfloat16 [16384, 4096], P('seq', 'tp')
- grad_taps: float32 [3, 4, 4096], P(None, None, 'tp')
- grad_tables: float32 [2, 1024, 4096], P(None, None, 'tp')
- grad_gain: float32 [4096], P('tp')
- grad_weight: float32 [4096, 4096], P('tp', 'seq')
Inputs may be any that keep to these rules, and one draw needn't show every extreme that they name: `log_decay`: each entry is the logarithm (at most 0) of one head's state decay at one token.
All inputs are finite; a program needn't handle non-finite values.
Results may differ from a plain program's by a relative error of at most 0.02.
Values may be sent and summed in bfloat16 or wider, within the bound.
A program may use at most 128 MiB of HBM per device.

v0:
```python
import jax
import jax.numpy as jnp
from jax import lax
from jax.sharding import PartitionSpec as P

HIGHEST = lax.Precision.HIGHEST


def shifted(x, axis, by):
    length = lax.axis_size(axis)
    pairs = [(i, i + by) for i in range(length) if 0 <= i + by < length]
    return lax.ppermute(x, axis, pairs)


def entering(log_total, state, axis, reverse):
    length = lax.axis_size(axis)
    step = -1 if reverse else 1
    heads, rows, cols = state.shape
    total_rows = jnp.broadcast_to(log_total[:, None, None], (heads, 8, cols))
    packed = shifted(jnp.concatenate([state, total_rows], axis=1), axis, step)
    distance = 1
    while distance < length:
        far = shifted(packed, axis, step * distance)
        near_total = packed[:, rows : rows + 1, :]
        packed = jnp.concatenate(
            [
                jnp.exp(near_total) * far[:, :rows, :] + packed[:, :rows, :],
                far[:, rows:, :] + packed[:, rows:, :],
            ],
            axis=1,
        )
        distance *= 2
    return packed[:, :rows, :]


def on_device(
    query_raw,
    key_raw,
    value_raw,
    conv_taps,
    layout_boxes,
    box_tables,
    log_decay,
    norm_gain,
    out_weight,
    grad_output,
):
    row_count, feat_width = query_raw.shape
    head_count = log_decay.shape[0]
    head_size = feat_width // head_count
    kernel = conv_taps.shape[1]
    buckets = box_tables.shape[1]
    feature_scale = head_size ** (-0.5)
    stacked = jnp.stack([query_raw, key_raw, value_raw])
    rim_rows = shifted(stacked[:, row_count - (kernel - 1) :, :], "seq", 1)
    padded = jnp.concatenate([rim_rows, stacked], axis=1).astype(jnp.float32)
    conved = jnp.zeros((3, row_count, feat_width), jnp.float32)
    for tap_step in range(kernel):
        conved = (
            conved
            + conv_taps[:, tap_step, None, :]
            * padded[:, kernel - 1 - tap_step : kernel - 1 - tap_step + row_count, :]
        )
    bucket_ids = jnp.arange(buckets, dtype=jnp.int32)

    def count_table(first, second):
        return (first[:, None] == bucket_ids[None, :]).astype(jnp.bfloat16) + (
            second[:, None] == bucket_ids[None, :]
        ).astype(jnp.bfloat16)

    hot_x = count_table(layout_boxes[0], layout_boxes[2])
    hot_y = count_table(layout_boxes[1], layout_boxes[3])
    layout = jnp.dot(hot_x, box_tables[0], preferred_element_type=jnp.float32) + jnp.dot(
        hot_y, box_tables[1], preferred_element_type=jnp.float32
    )
    query_feat = (feature_scale * (conved[0] + layout)).astype(jnp.bfloat16)
    key_feat = (conved[1] + layout).astype(jnp.bfloat16)
    value_feat = conved[2].astype(jnp.bfloat16)

    def split_heads(matrix):
        return matrix.reshape(row_count, head_count, head_size).transpose(1, 0, 2)

    def join_heads(blocks):
        return blocks.transpose(1, 0, 2).reshape(row_count, feat_width)

    query_heads = split_heads(query_feat)
    key_heads = split_heads(key_feat)
    value_heads = split_heads(value_feat)
    decay_sum = jnp.cumsum(log_decay, axis=1)
    decay_total = decay_sum[:, -1]
    head_decay = jnp.exp(decay_sum)[:, :, None]
    tail_decay = jnp.exp(decay_total[:, None] - decay_sum)[:, :, None]
    positions = jnp.arange(row_count, dtype=jnp.int32)
    causal_mask = positions[:, None] >= positions[None, :]
    decay_mask = jnp.where(
        causal_mask[None],
        jnp.exp(jnp.minimum(decay_sum[:, :, None] - decay_sum[:, None, :], 0.0)),
        0.0,
    )
    local_state = jnp.einsum("hsi,hsj->hij", key_heads * tail_decay, value_heads, precision=HIGHEST)
    incoming = entering(decay_total, local_state, "seq", False)
    scores = decay_mask * jnp.einsum(
        "hti,hsi->hts", query_heads, key_heads, preferred_element_type=jnp.float32
    )
    attended = jnp.einsum("hts,hsj->htj", scores, value_heads, precision=HIGHEST)
    attended = attended + head_decay * jnp.einsum(
        "hti,hij->htj", query_heads, incoming, precision=HIGHEST
    )
    inverse = lax.rsqrt(jnp.mean(attended * attended, axis=-1, keepdims=True) + 1e-06)
    unit_norm = attended * inverse
    gain_heads = norm_gain.reshape(head_count, 1, head_size)
    normed = join_heads(unit_norm * gain_heads).astype(jnp.bfloat16)
    partial_sum = jnp.dot(
        normed,
        lax.all_gather(out_weight, "seq", axis=1, tiled=True),
        preferred_element_type=jnp.float32,
    )
    layer_out = lax.psum_scatter(
        partial_sum.astype(jnp.bfloat16), "tp", scatter_dimension=1, tiled=True
    )
    cotangent = lax.all_gather(grad_output, "tp", axis=1, tiled=True)
    contract_last = (((1,), (1,)), ((), ()))
    grad_normed_sum = lax.dot_general(
        cotangent,
        lax.all_gather(out_weight, "seq", axis=1, tiled=True),
        contract_last,
        preferred_element_type=jnp.float32,
    )
    grad_normed = grad_normed_sum.astype(jnp.bfloat16)
    contract_first = (((0,), (0,)), ((), ()))
    weight_terms = lax.dot_general(
        normed, cotangent, contract_first, preferred_element_type=jnp.float32
    )
    grad_heads = split_heads(grad_normed).astype(jnp.float32)
    gain_terms = jnp.sum(grad_heads * unit_norm, axis=1).reshape(feat_width)
    grad_unit = grad_heads * gain_heads
    grad_attended = inverse * (
        grad_unit - unit_norm * jnp.mean(grad_unit * unit_norm, axis=-1, keepdims=True)
    )
    back_state = jnp.einsum(
        "hti,htj->hij", query_heads * head_decay, grad_attended, precision=HIGHEST
    )
    later_state = entering(decay_total, back_state, "seq", True)
    seq_count = lax.axis_size("seq")
    col_block = weight_terms.shape[1] // seq_count
    weight_parts = (
        weight_terms.astype(jnp.bfloat16)
        .reshape(feat_width, seq_count, col_block)
        .transpose(1, 0, 2)
    )
    weight_parts, later_state = lax.optimization_barrier((weight_parts, later_state))
    grad_scores = decay_mask * jnp.einsum(
        "htj,hsj->hts", grad_attended, value_heads, precision=HIGHEST
    )
    grad_qh = jnp.einsum(
        "hts,hsi->hti", grad_scores, key_heads, precision=HIGHEST
    ) + head_decay * jnp.einsum("htj,hij->hti", grad_attended, incoming, precision=HIGHEST)
    grad_kh = jnp.einsum(
        "hts,hti->hsi", grad_scores, query_heads, precision=HIGHEST
    ) + tail_decay * jnp.einsum("hsj,hij->hsi", value_heads, later_state, precision=HIGHEST)
    grad_vh = jnp.einsum(
        "hts,htj->hsj", scores, grad_attended, precision=HIGHEST
    ) + tail_decay * jnp.einsum("hsi,hij->hsj", key_heads, later_state, precision=HIGHEST)
    grad_pre = jnp.stack(
        [feature_scale * join_heads(grad_qh), join_heads(grad_kh), join_heads(grad_vh)]
    )
    next_rows = shifted(grad_pre[:, : kernel - 1, :], "seq", -1)
    extended = jnp.concatenate([grad_pre, next_rows], axis=1)
    grad_inputs = jnp.zeros((3, row_count, feat_width), jnp.float32)
    for tap_step in range(kernel):
        grad_inputs = (
            grad_inputs
            + conv_taps[:, tap_step, None, :] * extended[:, tap_step : tap_step + row_count, :]
        )
    tap_terms = jnp.stack(
        [
            jnp.sum(
                grad_pre * padded[:, kernel - 1 - tap_step : kernel - 1 - tap_step + row_count, :],
                axis=1,
            )
            for tap_step in range(kernel)
        ],
        axis=1,
    )
    grad_layout = (grad_pre[0] + grad_pre[1]).astype(jnp.bfloat16)
    table_terms = jnp.stack(
        [
            lax.dot_general(hot_x, grad_layout, contract_first, preferred_element_type=jnp.float32),
            lax.dot_general(hot_y, grad_layout, contract_first, preferred_element_type=jnp.float32),
        ]
    )
    table_rows = 2 * buckets
    tap_rows = 3 * kernel
    packed = jnp.concatenate(
        [
            table_terms.astype(jnp.bfloat16).reshape(table_rows, feat_width),
            tap_terms.astype(jnp.bfloat16).reshape(tap_rows, feat_width),
            gain_terms.astype(jnp.bfloat16).reshape(1, feat_width),
        ]
    )
    packed, layer_out, weight_parts = lax.optimization_barrier((packed, layer_out, weight_parts))
    summed = lax.psum(packed, "seq").astype(jnp.float32)
    weight_parts = lax.all_to_all(weight_parts, "seq", 0, 0, tiled=True)
    grad_weight = jnp.sum(weight_parts.astype(jnp.float32), axis=0)
    grad_tables = summed[:table_rows].reshape(2, buckets, feat_width)
    grad_taps = summed[table_rows : table_rows + tap_rows].reshape(3, kernel, feat_width)
    grad_gain = summed[table_rows + tap_rows]
    grad_query = grad_inputs[0].astype(jnp.bfloat16)
    grad_key = grad_inputs[1].astype(jnp.bfloat16)
    grad_value = grad_inputs[2].astype(jnp.bfloat16)
    return (
        layer_out,
        grad_query,
        grad_key,
        grad_value,
        grad_taps,
        grad_tables,
        grad_gain,
        grad_weight,
    )


def solution(mesh):
    return jax.shard_map(
        on_device,
        mesh=mesh,
        in_specs=(
            P("seq", "tp"),
            P("seq", "tp"),
            P("seq", "tp"),
            P(None, None, "tp"),
            P(None, "seq"),
            P(None, None, "tp"),
            P("tp", "seq"),
            P("tp"),
            P("tp", "seq"),
            P("seq", "tp"),
        ),
        out_specs=(
            P("seq", "tp"),
            P("seq", "tp"),
            P("seq", "tp"),
            P("seq", "tp"),
            P(None, None, "tp"),
            P(None, None, "tp"),
            P("tp"),
            P("tp", "seq"),
        ),
        check_vma=False,
    )
```

profile of v0, /device:TPU:2, one launch (start us, length us, event | category | flops | bytes accessed | tf_op | source)
XLA Modules:
  0.0 490.2 jit_solution(6953520611271623817)
XLA Ops:
  31.8 4.4 collective-permute-start.1
  36.2 5.0 %collective-permute-done.1 = f32[4,136,128]{2,1,0:T(8,128)S(1)} collective-permute-done((f32[4,136,128]{2,1,0:T(8,128)S(1)}, f32[4,136,128]{2,1,0:T(8,128)S(1)}, u32[]{:S(2)}, u32[]{:S(2)}) %collective-permute-start.1) | collective-permute-done | bytes 278560 | tf_op jit(solution)/shard_map/ppermute | solution.py:12
  41.3 4.4 collective-permute-start.2
  45.7 4.3 collective-permute-done.2
  50.0 6.0 %collective-permute-start.3 = (f32[4,136,128]{2,1,0:T(8,128)S(1)}, f32[4,136,128]{2,1,0:T(8,128)S(1)}, u32[]{:S(2)}, u32[]{:S(2)}) collective-permute-start(f32[4,136,128]{2,1,0:T(8,128)S(1)} %pad_maximum_fusion.7), channel_id=1, source_target_pairs={{0,16},{8,24},{16,32},{24,40},{32,48},{40,56},{48,64},{56,72},{64,... | collective-permute-start | bytes 835592 | tf_op jit(solution)/shard_map/ppermute | solution.py:12
  60.1 12.8 %collective-permute-start.4 = (f32[4,136,128]{2,1,0:T(8,128)S(1)}, f32[4,136,128]{2,1,0:T(8,128)S(1)}, u32[]{:S(2)}, u32[]{:S(2)}) collective-permute-start(f32[4,136,128]{2,1,0:T(8,128)S(1)} %pad_maximum_fusion.8), channel_id=1, source_target_pairs={{0,32},{8,40},{16,48},{24,56},{32,64},{40,72},{48,80},{56,88},{64,... | collective-permute-start | bytes 835592 | tf_op jit(solution)/shard_map/ppermute | solution.py:12
  72.9 4.7 collective-permute-done.4
  77.7 6.3 %collective-permute-start.5 = (f32[4,136,128]{2,1,0:T(8,128)S(1)}, f32[4,136,128]{2,1,0:T(8,128)S(1)}, u32[]{:S(2)}, u32[]{:S(2)}) collective-permute-start(f32[4,136,128]{2,1,0:T(8,128)S(1)} %pad_maximum_fusion.9), channel_id=1, source_target_pairs={{0,64},{8,72},{16,80},{24,88},{32,96},{40,104},{48,112},{56,120},{... | collective-permute-start | bytes 835592 | tf_op jit(solution)/shard_map/ppermute | solution.py:12
  84.2 4.3 collective-permute-done.5
  88.5 24.3 %collective-permute-start.6 = (f32[4,136,128]{2,1,0:T(8,128)S(1)}, f32[4,136,128]{2,1,0:T(8,128)S(1)}, u32[]{:S(2)}, u32[]{:S(2)}) collective-permute-start(f32[4,136,128]{2,1,0:T(8,128)S(1)} %pad_maximum_fusion.10), channel_id=1, source_target_pairs={{0,128},{8,136},{16,144},{24,152},{32,160},{40,168},{48,176},{56,1... | collective-permute-start | bytes 835592 | tf_op jit(solution)/shard_map/ppermute | solution.py:12
  113.6 4.9 %collective-permute-done.6 = f32[4,136,128]{2,1,0:T(8,128)S(1)} collective-permute-done((f32[4,136,128]{2,1,0:T(8,128)S(1)}, f32[4,136,128]{2,1,0:T(8,128)S(1)}, u32[]{:S(2)}, u32[]{:S(2)}) %collective-permute-start.6) | collective-permute-done | bytes 278560 | tf_op jit(solution)/shard_map/ppermute | solution.py:12
  123.9 28.5 %all-gather.5.cloned.1.call-done = bf16[512,4096]{1,0:T(8,128)(2,1)} async-done(((bf16[512,128]{1,0:T(8,128)(2,1)}), bf16[512,4096]{1,0:T(8,128)(2,1)}) %all-gather.5.cloned.1.call-update) | async-done | bytes 4194320 | tf_op jit(solution)/shard_map/all_gather | solution.py:125
  152.5 6.0 %convolution_convert_fusion.4 = bf16[512,512]{0,1:T(8,128)(2,1)S(1)} fusion(bf16[512,4096]{1,0:T(8,128)(2,1)} %all-gather.3.cloned.1.call-done, bf16[512,4096]{1,0:T(8,128)(2,1)} %all-gather.5.cloned.1.call-done), kind=kOutput, calls=%fused_computation.70 | convolution fusion | flops 2147745792 | bytes 8912896 | tf_op jit(solution)/shard_map/dot_general | solution.py:123
  167.2 4.2 collective-permute-done.7
  172.8 4.5 convolution_convert_fusion
  183.0 5.8 %fusion.41 = f32[512,4,128]{0,2,1:T(8,128)S(1)} fusion(f32[4,512,512]{2,1,0:T(8,128)} %copy-done.7, f32[4,512]{1,0:T(4,128)S(1)} %bitcast.265, pred[512,512]{1,0:T(8,128)(4,1)} %copy-done.18, f32[4,512,128]{1,2,0:T(8,128)S(1)} %get-tuple-element.57, f32[4,512]{1,0:T(4,128)S(1)} %broadcast_multiply_fusion, f32[4,128]{1,0:T(4,128)S(1)} %bitcast.254, ...), kind=kOutput, calls=%fused_computation.56 | convolution fusion | flops 1616379904 | bytes 7104512 | tf_op jit(solution)/shard_map/hts,htj->hsj/dot_general | solution.py:161
  195.2 6.3 %collective-permute-done.10 = f32[4,136,128]{2,1,0:T(8,128)S(1)} collective-permute-done((f32[4,136,128]{2,1,0:T(8,128)S(1)}, f32[4,136,128]{2,1,0:T(8,128)S(1)}, u32[]{:S(2)}, u32[]{:S(2)}) %collective-permute-start.10) | collective-permute-done | bytes 278560 | tf_op jit(solution)/shard_map/ppermute | solution.py:12
  206.4 10.0 %collective-permute-done.11 = f32[4,136,128]{2,1,0:T(8,128)S(1)} collective-permute-done((f32[4,136,128]{2,1,0:T(8,128)S(1)}, f32[4,136,128]{2,1,0:T(8,128)S(1)}, u32[]{:S(2)}, u32[]{:S(2)}) %collective-permute-start.11) | collective-permute-done | bytes 278560 | tf_op jit(solution)/shard_map/ppermute | solution.py:12
  220.8 10.7 %collective-permute-done.12 = f32[4,136,128]{2,1,0:T(8,128)S(1)} collective-permute-done((f32[4,136,128]{2,1,0:T(8,128)S(1)}, f32[4,136,128]{2,1,0:T(8,128)S(1)}, u32[]{:S(2)}, u32[]{:S(2)}) %collective-permute-start.12) | collective-permute-done | bytes 278560 | tf_op jit(solution)/shard_map/ppermute | solution.py:12
  247.9 8.4 %multiply_reduce_fusion.3 = (bf16[3,512]{1,0:T(4,128)(2,1)S(1)}, bf16[3,512]{1,0:T(4,128)(2,1)S(1)}, bf16[3,512]{1,0:T(4,128)(2,1)S(1)}, bf16[3,512]{1,0:T(4,128)(2,1)S(1)}, bf16[3,512,512]{1,2,0:T(8,128)(2,1)}) fusion(f32[3,515,512]{1,2,0:T(8,128)S(1)} %copy-done.1, f32[1,512,512]{1,2,0:T(8,128)S(1)} %bitcast.225, f32[1,512,512]{1,2,0:T(8,128)S(1)} %bitcast.218, ...), kind=kLoop, calls=%fused_computation.19 | loop fusion | flops 14149632 | bytes 26775552 | tf_op jit(solution)/shard_map/reduce_sum | solution.py:177
  256.3 11.3 %concatenate.50 = bf16[2061,512]{1,0:T(8,128)(2,1)} concatenate(bf16[2048,512]{1,0:T(8,128)(2,1)} %bitcast.226, bf16[12,512]{1,0:T(8,128)(2,1)S(1)} %convert_element_type.123, bf16[1,512]{1,0:T(2,128)(2,1)S(1)} %bitcast.268), dimensions={0} | concatenate | bytes 4220928 | tf_op jit(solution)/shard_map/concatenate | solution.py:194
  267.7 16.4 %all-to-all-start = ((bf16[32,512,128]{2,1,0:T(8,128)(2,1)}), bf16[32,512,128]{2,1,0:T(8,128)(2,1)}, u32[]{:S(2)}, u32[]{:S(2)}) async-start(bf16[32,512,128]{2,1,0:T(8,128)(2,1)} %bitcast.222), calls=%async_computation.1 | async-start | bytes 8388608 | tf_op jit(solution)/shard_map/all_to_all | solution.py:203
  288.6 184.5 %all-reduce.2.cloned.1.call-done = bf16[2061,512]{1,0:T(8,128)(2,1)} async-done(((bf16[2061,512]{1,0:T(8,128)(2,1)}), bf16[2061,512]{1,0:T(8,128)(2,1)}) %all-reduce.2.cloned.1.call-update) | async-done | bytes 2110480 | tf_op jit(solution)/shard_map/psum | solution.py:202
  474.4 4.2 slice.316
  (175 shorter events, 93.2 us)
Async XLA Ops:
  7.2 116.7 %all-gather.3.cloned.1.call-start = ((), (), s32[]{:S(2)}) async-start(), calls=%async_computation.2 | async-start | bytes 4718592 | tf_op jit(solution)/shard_map/all_gather | solution.py:121
  7.9 144.5 %all-gather.5.cloned.1.call-start = ((), (), s32[]{:S(2)}) async-start(), calls=%async_computation.3 | async-start | bytes 4325376 | tf_op jit(solution)/shard_map/all_gather | solution.py:125
  11.9 11.8 %collective-permute-start = (bf16[3,3,512]{1,2,0:T(8,128)(2,1)S(1)}, bf16[3,3,512]{1,2,0:T(8,128)(2,1)S(1)}, u32[]{:S(2)}, u32[]{:S(2)}) collective-permute-start(bf16[3,3,512]{1,2,0:T(8,128)(2,1)S(1)} %pad_maximum_fusion.5), channel_id=1, source_target_pairs={{0,8},{8,16},{16,24},{24,32},{32,40},{40,48},{48,56},{56,64},{64,7... | collective-permute-start | bytes 27656 | tf_op jit(solution)/shard_map/ppermute | solution.py:12
  15.5 252.2 %reduce-scatter.2.cloned.1.call-start = ((), (), s32[]{:S(2)}) async-start(), calls=%async_computation.4 | async-start | bytes 4718592 | tf_op jit(solution)/shard_map/reduce_scatter | solution.py:118
  29.6 129.3 %copy-start.9 = (bf16[512,512]{0,1:T(8,128)(2,1)}, bf16[512,512]{0,1:T(8,128)(2,1)S(1)}, u32[]{:S(2)}) copy-start(bf16[512,512]{0,1:T(8,128)(2,1)S(1)} %get-tuple-element.58) | copy-start | bytes 1572868
  31.8 9.4 %collective-permute-start.1 = (f32[4,136,128]{2,1,0:T(8,128)S(1)}, f32[4,136,128]{2,1,0:T(8,128)S(1)}, u32[]{:S(2)}, u32[]{:S(2)}) collective-permute-start(f32[4,136,128]{2,1,0:T(8,128)S(1)} %pad_maximum_fusion.4), channel_id=1, source_target_pairs={{0,8},{8,16},{16,24},{24,32},{32,40},{40,48},{48,56},{56,64},{64,7... | collective-permute-start | bytes 835592 | tf_op jit(solution)/shard_map/ppermute | solution.py:12
  41.3 8.7 %collective-permute-start.2 = (f32[4,136,128]{2,1,0:T(8,128)S(1)}, f32[4,136,128]{2,1,0:T(8,128)S(1)}, u32[]{:S(2)}, u32[]{:S(2)}) collective-permute-start(f32[4,136,128]{2,1,0:T(8,128)S(1)} %collective-permute-done.1), channel_id=1, source_target_pairs={{0,8},{8,16},{16,24},{24,32},{32,40},{40,48},{48,56},{56,64},{64,7... | collective-permute-start | bytes 835592 | tf_op jit(solution)/shard_map/ppermute | solution.py:12
  50.0 10.1 %collective-permute-start.3 = (f32[4,136,128]{2,1,0:T(8,128)S(1)}, f32[4,136,128]{2,1,0:T(8,128)S(1)}, u32[]{:S(2)}, u32[]{:S(2)}) collective-permute-start(f32[4,136,128]{2,1,0:T(8,128)S(1)} %pad_maximum_fusion.7), channel_id=1, source_target_pairs={{0,16},{8,24},{16,32},{24,40},{32,48},{40,56},{48,64},{56,72},{64,... | collective-permute-start | bytes 835592 | tf_op jit(solution)/shard_map/ppermute | solution.py:12
  60.1 17.5 %collective-permute-start.4 = (f32[4,136,128]{2,1,0:T(8,128)S(1)}, f32[4,136,128]{2,1,0:T(8,128)S(1)}, u32[]{:S(2)}, u32[]{:S(2)}) collective-permute-start(f32[4,136,128]{2,1,0:T(8,128)S(1)} %pad_maximum_fusion.8), channel_id=1, source_target_pairs={{0,32},{8,40},{16,48},{24,56},{32,64},{40,72},{48,80},{56,88},{64,... | collective-permute-start | bytes 835592 | tf_op jit(solution)/shard_map/ppermute | solution.py:12
  77.7 10.7 %collective-permute-start.5 = (f32[4,136,128]{2,1,0:T(8,128)S(1)}, f32[4,136,128]{2,1,0:T(8,128)S(1)}, u32[]{:S(2)}, u32[]{:S(2)}) collective-permute-start(f32[4,136,128]{2,1,0:T(8,128)S(1)} %pad_maximum_fusion.9), channel_id=1, source_target_pairs={{0,64},{8,72},{16,80},{24,88},{32,96},{40,104},{48,112},{56,120},{... | collective-permute-start | bytes 835592 | tf_op jit(solution)/shard_map/ppermute | solution.py:12
  84.1 35.0 %copy-start.18 = (pred[512,512]{1,0:T(8,128)(4,1)}, pred[512,512]{1,0:T(8,128)(4,1)S(1)}, u32[]{:S(2)}) copy-start(pred[512,512]{1,0:T(8,128)(4,1)S(1)} %iota_compare_fusion.4) | copy-start | bytes 786436
  88.5 30.0 %collective-permute-start.6 = (f32[4,136,128]{2,1,0:T(8,128)S(1)}, f32[4,136,128]{2,1,0:T(8,128)S(1)}, u32[]{:S(2)}, u32[]{:S(2)}) collective-permute-start(f32[4,136,128]{2,1,0:T(8,128)S(1)} %pad_maximum_fusion.10), channel_id=1, source_target_pairs={{0,128},{8,136},{16,144},{24,152},{32,160},{40,168},{48,176},{56,1... | collective-permute-start | bytes 835592 | tf_op jit(solution)/shard_map/ppermute | solution.py:12
  122.8 70.4 %copy-start.2 = (f32[4,512,128]{1,2,0:T(8,128)}, f32[4,512,128]{1,2,0:T(8,128)S(1)}, u32[]{:S(2)}) copy-start(f32[4,512,128]{1,2,0:T(8,128)S(1)} %get-tuple-element.57) | copy-start | bytes 3145732
  158.4 34.8 %copy-start.5 = (bf16[512,512]{0,1:T(8,128)(2,1)}, bf16[512,512]{0,1:T(8,128)(2,1)S(1)}, u32[]{:S(2)}) copy-start(bf16[512,512]{0,1:T(8,128)(2,1)S(1)} %convolution_convert_fusion.4) | copy-start | bytes 1572868
  160.4 11.0 %collective-permute-start.7 = (f32[4,136,128]{2,1,0:T(8,128)S(1)}, f32[4,136,128]{2,1,0:T(8,128)S(1)}, u32[]{:S(2)}, u32[]{:S(2)}) collective-permute-start(f32[4,136,128]{2,1,0:T(8,128)S(1)} %pad_maximum_fusion.3), channel_id=1, source_target_pairs={{8,0},{16,8},{24,16},{32,24},{40,32},{48,40},{56,48},{64,56},{72,6... | collective-permute-start | bytes 835592 | tf_op jit(solution)/shard_map/ppermute | solution.py:12
  171.4 8.5 %collective-permute-start.8 = (f32[4,136,128]{2,1,0:T(8,128)S(1)}, f32[4,136,128]{2,1,0:T(8,128)}, u32[]{:S(2)}, u32[]{:S(2)}) collective-permute-start(f32[4,136,128]{2,1,0:T(8,128)S(1)} %collective-permute-done.7), channel_id=1, source_target_pairs={{8,0},{16,8},{24,16},{32,24},{40,32},{48,40},{56,48},{64,56},{72,6... | collective-permute-start | bytes 835592 | tf_op jit(solution)/shard_map/ppermute | solution.py:12
  181.7 9.9 %collective-permute-start.9 = (f32[4,136,128]{2,1,0:T(8,128)S(1)}, f32[4,136,128]{2,1,0:T(8,128)S(1)}, u32[]{:S(2)}, u32[]{:S(2)}) collective-permute-start(f32[4,136,128]{2,1,0:T(8,128)S(1)} %pad_maximum_fusion.11), channel_id=1, source_target_pairs={{16,0},{24,8},{32,16},{40,24},{48,32},{56,40},{64,48},{72,56},{80,... | collective-permute-start | bytes 835592 | tf_op jit(solution)/shard_map/ppermute | solution.py:12
  191.8 9.8 %collective-permute-start.10 = (f32[4,136,128]{2,1,0:T(8,128)S(1)}, f32[4,136,128]{2,1,0:T(8,128)S(1)}, u32[]{:S(2)}, u32[]{:S(2)}) collective-permute-start(f32[4,136,128]{2,1,0:T(8,128)S(1)} %pad_maximum_fusion.12), channel_id=1, source_target_pairs={{32,0},{40,8},{48,16},{56,24},{64,32},{72,40},{80,48},{88,56},{96,... | collective-permute-start | bytes 835592 | tf_op jit(solution)/shard_map/ppermute | solution.py:12
  201.6 14.8 %collective-permute-start.11 = (f32[4,136,128]{2,1,0:T(8,128)S(1)}, f32[4,136,128]{2,1,0:T(8,128)S(1)}, u32[]{:S(2)}, u32[]{:S(2)}) collective-permute-start(f32[4,136,128]{2,1,0:T(8,128)S(1)} %pad_maximum_fusion.13), channel_id=1, source_target_pairs={{64,0},{72,8},{80,16},{88,24},{96,32},{104,40},{112,48},{120,56},{... | collective-permute-start | bytes 835592 | tf_op jit(solution)/shard_map/ppermute | solution.py:12
  202.9 15.1 %copy-start.10 = (bf16[512,512]{0,1:T(8,128)(2,1)S(1)}, bf16[512,512]{0,1:T(8,128)(2,1)}, u32[]{:S(2)}) copy-start(bf16[512,512]{0,1:T(8,128)(2,1)} %copy-done.9) | copy-start | bytes 1572868
  216.5 15.0 %collective-permute-start.12 = (f32[4,136,128]{2,1,0:T(8,128)S(1)}, f32[4,136,128]{2,1,0:T(8,128)S(1)}, u32[]{:S(2)}, u32[]{:S(2)}) collective-permute-start(f32[4,136,128]{2,1,0:T(8,128)S(1)} %pad_maximum_fusion.14), channel_id=1, source_target_pairs={{128,0},{136,8},{144,16},{152,24},{160,32},{168,40},{176,48},{184,... | collective-permute-start | bytes 835592 | tf_op jit(solution)/shard_map/ppermute | solution.py:12
  237.9 6.4 %collective-permute-start.13 = (f32[3,3,512]{2,1,0:T(4,128)S(1)}, f32[3,3,512]{2,1,0:T(4,128)S(1)}, u32[]{:S(2)}, u32[]{:S(2)}) collective-permute-start(f32[3,3,512]{2,1,0:T(4,128)S(1)} %copy.98), channel_id=1, source_target_pairs={{8,0},{16,8},{24,16},{32,24},{40,32},{48,40},{56,48},{64,56},{72,6... | collective-permute-start | bytes 55304 | tf_op jit(solution)/shard_map/ppermute | solution.py:12
  267.7 212.3 %all-to-all-start = ((bf16[32,512,128]{2,1,0:T(8,128)(2,1)}), bf16[32,512,128]{2,1,0:T(8,128)(2,1)}, u32[]{:S(2)}, u32[]{:S(2)}) async-start(bf16[32,512,128]{2,1,0:T(8,128)(2,1)} %bitcast.222), calls=%async_computation.1 | async-start | bytes 8388608 | tf_op jit(solution)/shard_map/all_to_all | solution.py:203
  284.1 189.0 %all-reduce.2.cloned.1.call-start = ((), (), s32[]{:S(2)}) async-start(), calls=%async_computation.5 | async-start | bytes 4227072 | tf_op jit(solution)/shard_map/psum | solution.py:202
  (21 other events, 112.4 us)
Sparse Core Ops, SparseCore 0:
  9.8 36.5 all-gather.2
  48.9 103.5 all-gather.4
  177.4 35.0 reduce-scatter.1
  288.1 184.9 all-reduce.1
where the time goes:
time: 497 us; the launch traced here: 490 us
  waiting for transfers between devices  283 us (57%)
  starting transfers between devices  87.9 us (18%)
  matrix products  44.2 us (9%)
  local copies, waits for them, and re-layouts  34.9 us (7%)
  other arithmetic  25.7 us (5%)
  between operations  14.9 us (3%)
    psum x1, waiting for transfers between devices, on_device(): summed = lax.psum(packed, 'seq').astype(jnp.float32)  184 us
    ppermute x14, starting transfers between devices, shifted(): return lax.ppermute(x, axis, pairs)  71.4 us
    ppermute x14, waiting for transfers between devices, shifted(): return lax.ppermute(x, axis, pairs)  68.3 us
    all_gather x1, waiting for transfers between devices, on_device(): lax.all_gather(out_weight, 'seq', axis=1, tiled=True)  28.5 us
    all_to_all x1, starting transfers between devices, on_device(): weight_parts = lax.all_to_all(weight_parts, 'seq', 0, 0, tiled=True)  16.4 us
    concatenate x1, local copies, waits for them, and re-layouts, on_device(): jnp.concatenate([table_terms.astype(jnp.bfloat16).reshape(table_rows, fea...  11.3 us
  transfers between devices with their start and end apart: 19, of which 16 were waited for; matrix products, arithmetic and copies ran while one was open for 19% of the time, Pallas kernels for 0%

commit v1 on v0

--- a/solution.py
+++ b/solution.py
@@ -199,7 +199,7 @@
         ]
     )
     packed, layer_out, weight_parts = lax.optimization_barrier((packed, layer_out, weight_parts))
-    summed = lax.psum(packed, "seq").astype(jnp.float32)
+    summed = jnp.sum(lax.all_gather(packed, "seq"), axis=0).astype(jnp.float32)
     weight_parts = lax.all_to_all(weight_parts, "seq", 0, 0, tiled=True)
     grad_weight = jnp.sum(weight_parts.astype(jnp.float32), axis=0)
     grad_tables = summed[:table_rows].reshape(2, buckets, feat_width)

time: 497 us -> 818 us (1.65)
  waiting for transfers between devices: 283 us -> 584 us
  other arithmetic: 25.7 us -> 47.7 us
    all_gather x0 -> x1, waiting for transfers between devices: none -> 366 us  [on_device(): summed = jnp.sum(lax.all_gather(packed, 'seq'), axis=0).astype(jnp.float32)]
    psum x1 -> x0, waiting for transfers between devices: 184 us -> none  [on_device(): summed = lax.psum(packed, 'seq').astype(jnp.float32)]
    all_to_all x1, waiting for transfers between devices: 0.01 us -> 121 us  [on_device(): weight_parts = lax.all_to_all(weight_parts, 'seq', 0, 0, tiled=True)]
    reduce_sum x0 -> x1, other arithmetic: none -> 21.9 us  [on_device(): summed = jnp.sum(lax.all_gather(packed, 'seq'), axis=0).astype(jnp.float32)]
  transfers between devices with their start and end apart: 19 -> 19, of which waited for: 16 -> 17; matrix products, arithmetic and copies ran while one was open for 19% -> 11% of each run, Pallas kernels for 0% -> 0%
where the time goes in v1:
time: 818 us; the launch traced here: 810 us
  waiting for transfers between devices  584 us (71%)
  starting transfers between devices  88.4 us (11%)
  other arithmetic  47.7 us (6%)
  matrix products  44.2 us (5%)
  local copies, waits for them, and re-layouts  31.1 us (4%)
  between operations  14.9 us (2%)
    all_gather x1, waiting for transfers between devices, on_device(): summed = jnp.sum(lax.all_gather(packed, 'seq'), axis=0).astype(jnp.float32)  366 us
    all_to_all x1, waiting for transfers between devices, on_device(): weight_parts = lax.all_to_all(weight_parts, 'seq', 0, 0, tiled=True)  121 us
    ppermute x14, starting transfers between devices, shifted(): return lax.ppermute(x, axis, pairs)  71.4 us
    ppermute x14, waiting for transfers between devices, shifted(): return lax.ppermute(x, axis, pairs)  68.1 us
    all_gather x1, waiting for transfers between devices, on_device(): lax.all_gather(out_weight, 'seq', axis=1, tiled=True)  28.5 us
    reduce_sum x1, other arithmetic, on_device(): summed = jnp.sum(lax.all_gather(packed, 'seq'), axis=0).astype(jnp.float32)  21.9 us
    all_to_all x1, starting transfers between devices, on_device(): weight_parts = lax.all_to_all(weight_parts, 'seq', 0, 0, tiled=True)  16.9 us
  transfers between devices with their start and end apart: 19, of which 17 were waited for; matrix products, arithmetic and copies ran while one was open for 11% of the time, Pallas kernels for 0%

profile of v1, /device:TPU:2, one launch (start us, length us, event | category | flops | bytes accessed | tf_op | source)
XLA Modules:
  0.0 810.4 jit_solution(15780592282849066111)
XLA Ops:
  31.8 4.4 collective-permute-start.1
  36.2 5.0 collective-permute-done.1
  41.3 4.4 collective-permute-start.2
  45.7 4.3 collective-permute-done.2
  50.0 6.0 collective-permute-start.3
  60.1 12.8 %collective-permute-start.4 = (f32[4,136,128]{2,1,0:T(8,128)S(1)}, f32[4,136,128]{2,1,0:T(8,128)S(1)}, u32[]{:S(2)}, u32[]{:S(2)}) collective-permute-start(f32[4,136,128]{2,1,0:T(8,128)S(1)} %pad_maximum_fusion.8), channel_id=1, source_target_pairs={{0,32},{8,40},{16,48},{24,56},{32,64},{40,72},{48,80},{56,88},{64,... | collective-permute-start | bytes 835592 | tf_op jit(solution)/shard_map/ppermute | solution.py:12
  72.9 4.7 collective-permute-done.4
  77.7 6.4 collective-permute-start.5
  84.2 4.3 collective-permute-done.5
  88.5 24.3 %collective-permute-start.6 = (f32[4,136,128]{2,1,0:T(8,128)S(1)}, f32[4,136,128]{2,1,0:T(8,128)S(1)}, u32[]{:S(2)}, u32[]{:S(2)}) collective-permute-start(f32[4,136,128]{2,1,0:T(8,128)S(1)} %pad_maximum_fusion.10), channel_id=1, source_target_pairs={{0,128},{8,136},{16,144},{24,152},{32,160},{40,168},{48,176},{56,1... | collective-permute-start | bytes 835592 | tf_op jit(solution)/shard_map/ppermute | solution.py:12
  113.6 4.9 collective-permute-done.6
  123.9 28.5 %all-gather.8.cloned.1.call-done = bf16[512,4096]{1,0:T(8,128)(2,1)} async-done(((bf16[512,128]{1,0:T(8,128)(2,1)}), bf16[512,4096]{1,0:T(8,128)(2,1)}) %all-gather.8.cloned.1.call-update) | async-done | bytes 4194320 | tf_op jit(solution)/shard_map/all_gather | solution.py:125
  152.4 6.0 convolution_convert_fusion.4
  172.7 4.5 convolution_convert_fusion
  182.9 5.8 fusion.41
  195.1 6.3 collective-permute-done.10
  206.3 9.9 %collective-permute-done.11 = f32[4,136,128]{2,1,0:T(8,128)S(1)} collective-permute-done((f32[4,136,128]{2,1,0:T(8,128)S(1)}, f32[4,136,128]{2,1,0:T(8,128)S(1)}, u32[]{:S(2)}, u32[]{:S(2)}) %collective-permute-start.11) | collective-permute-done | bytes 278560 | tf_op jit(solution)/shard_map/ppermute | solution.py:12
  220.6 10.8 %collective-permute-done.12 = f32[4,136,128]{2,1,0:T(8,128)S(1)} collective-permute-done((f32[4,136,128]{2,1,0:T(8,128)S(1)}, f32[4,136,128]{2,1,0:T(8,128)S(1)}, u32[]{:S(2)}, u32[]{:S(2)}) %collective-permute-start.12) | collective-permute-done | bytes 278560 | tf_op jit(solution)/shard_map/ppermute | solution.py:12
  247.8 8.4 %multiply_reduce_fusion.3 = (bf16[3,512]{1,0:T(4,128)(2,1)S(1)}, bf16[3,512]{1,0:T(4,128)(2,1)S(1)}, bf16[3,512]{1,0:T(4,128)(2,1)S(1)}, bf16[3,512]{1,0:T(4,128)(2,1)S(1)}, bf16[3,512,512]{1,2,0:T(8,128)(2,1)}) fusion(f32[3,515,512]{1,2,0:T(8,128)S(1)} %copy-done.1, f32[1,512,512]{1,2,0:T(8,128)S(1)} %bitcast.226, f32[1,512,512]{1,2,0:T(8,128)S(1)} %bitcast.219, ...), kind=kLoop, calls=%fused_computation.19 | loop fusion | flops 14149632 | bytes 26775552 | tf_op jit(solution)/shard_map/reduce_sum | solution.py:177
  256.2 11.3 %concatenate.50 = bf16[2061,512]{1,0:T(8,128)(2,1)} concatenate(bf16[2048,512]{1,0:T(8,128)(2,1)} %bitcast.228, bf16[12,512]{1,0:T(8,128)(2,1)S(1)} %convert_element_type.125, bf16[1,512]{1,0:T(2,128)(2,1)S(1)} %bitcast.270), dimensions={0} | concatenate | bytes 4220928 | tf_op jit(solution)/shard_map/concatenate | solution.py:194
  267.6 16.9 %all-to-all-start = ((bf16[32,512,128]{2,1,0:T(8,128)(2,1)}), bf16[32,512,128]{2,1,0:T(8,128)(2,1)}, u32[]{:S(2)}, u32[]{:S(2)}) async-start(bf16[32,512,128]{2,1,0:T(8,128)(2,1)} %bitcast.223), calls=%async_computation.1 | async-start | bytes 8388608 | tf_op jit(solution)/shard_map/all_to_all | solution.py:203
  287.6 120.8 %all-to-all-done = bf16[32,512,128]{2,1,0:T(8,128)(2,1)} async-done(((bf16[32,512,128]{2,1,0:T(8,128)(2,1)}), bf16[32,512,128]{2,1,0:T(8,128)(2,1)}, u32[]{:S(2)}, u32[]{:S(2)}) %all-to-all-start) | async-done | bytes 4194336 | tf_op jit(solution)/shard_map/all_to_all | solution.py:203
  412.0 365.9 %all-gather.10.cloned.1.call-done = bf16[32,2061,512]{2,1,0:T(8,128)(2,1)} async-done(((bf16[1,2061,512]{2,1,0:T(8,128)(2,1)}), bf16[32,2061,512]{2,1,0:T(8,128)(2,1)}) %all-gather.10.cloned.1.call-update) | async-done | bytes 67534864 | tf_op jit(solution)/shard_map/all_gather | solution.py:202
  777.8 21.9 %reduce_sum.91 = bf16[2061,512]{1,0:T(8,128)(2,1)S(1)} reduce(bf16[32,2061,512]{2,1,0:T(8,128)(2,1)} %all-gather.10.cloned.1.call-done, bf16[]{:T(256)} %constant.15.clone.1), dimensions={0}, to_apply=%region_10.11 | reduce | flops 32712192 | bytes 69645312 | tf_op jit(solution)/shard_map/reduce_sum | solution.py:202
  (176 shorter events, 97.1 us)
Async XLA Ops:
  7.2 116.7 %all-gather.6.cloned.1.call-start = ((), (), s32[]{:S(2)}) async-start(), calls=%async_computation.2 | async-start | bytes 4718592 | tf_op jit(solution)/shard_map/all_gather | solution.py:121
  7.9 144.5 %all-gather.8.cloned.1.call-start = ((), (), s32[]{:S(2)}) async-start(), calls=%async_computation.3 | async-start | bytes 4325376 | tf_op jit(solution)/shard_map/all_gather | solution.py:125
  11.9 11.8 %collective-permute-start = (bf16[3,3,512]{1,2,0:T(8,128)(2,1)S(1)}, bf16[3,3,512]{1,2,0:T(8,128)(2,1)S(1)}, u32[]{:S(2)}, u32[]{:S(2)}) collective-permute-start(bf16[3,3,512]{1,2,0:T(8,128)(2,1)S(1)} %pad_maximum_fusion.5), channel_id=1, source_target_pairs={{0,8},{8,16},{16,24},{24,32},{32,40},{40,48},{48,56},{56,64},{64,7... | collective-permute-start | bytes 27656 | tf_op jit(solution)/shard_map/ppermute | solution.py:12
  15.5 252.1 %reduce-scatter.2.cloned.1.call-start = ((), (), s32[]{:S(2)}) async-start(), calls=%async_computation.4 | async-start | bytes 4718592 | tf_op jit(solution)/shard_map/reduce_scatter | solution.py:118
  29.6 129.3 %copy-start.9 = (bf16[512,512]{0,1:T(8,128)(2,1)}, bf16[512,512]{0,1:T(8,128)(2,1)S(1)}, u32[]{:S(2)}) copy-start(bf16[512,512]{0,1:T(8,128)(2,1)S(1)} %get-tuple-element.58) | copy-start | bytes 1572868
  31.8 9.4 %collective-permute-start.1 = (f32[4,136,128]{2,1,0:T(8,128)S(1)}, f32[4,136,128]{2,1,0:T(8,128)S(1)}, u32[]{:S(2)}, u32[]{:S(2)}) collective-permute-start(f32[4,136,128]{2,1,0:T(8,128)S(1)} %pad_maximum_fusion.4), channel_id=1, source_target_pairs={{0,8},{8,16},{16,24},{24,32},{32,40},{40,48},{48,56},{56,64},{64,7... | collective-permute-start | bytes 835592 | tf_op jit(solution)/shard_map/ppermute | solution.py:12
  41.3 8.7 %collective-permute-start.2 = (f32[4,136,128]{2,1,0:T(8,128)S(1)}, f32[4,136,128]{2,1,0:T(8,128)S(1)}, u32[]{:S(2)}, u32[]{:S(2)}) collective-permute-start(f32[4,136,128]{2,1,0:T(8,128)S(1)} %collective-permute-done.1), channel_id=1, source_target_pairs={{0,8},{8,16},{16,24},{24,32},{32,40},{40,48},{48,56},{56,64},{64,7... | collective-permute-start | bytes 835592 | tf_op jit(solution)/shard_map/ppermute | solution.py:12
  50.0 10.1 %collective-permute-start.3 = (f32[4,136,128]{2,1,0:T(8,128)S(1)}, f32[4,136,128]{2,1,0:T(8,128)S(1)}, u32[]{:S(2)}, u32[]{:S(2)}) collective-permute-start(f32[4,136,128]{2,1,0:T(8,128)S(1)} %pad_maximum_fusion.7), channel_id=1, source_target_pairs={{0,16},{8,24},{16,32},{24,40},{32,48},{40,56},{48,64},{56,72},{64,... | collective-permute-start | bytes 835592 | tf_op jit(solution)/shard_map/ppermute | solution.py:12
  60.1 17.5 %collective-permute-start.4 = (f32[4,136,128]{2,1,0:T(8,128)S(1)}, f32[4,136,128]{2,1,0:T(8,128)S(1)}, u32[]{:S(2)}, u32[]{:S(2)}) collective-permute-start(f32[4,136,128]{2,1,0:T(8,128)S(1)} %pad_maximum_fusion.8), channel_id=1, source_target_pairs={{0,32},{8,40},{16,48},{24,56},{32,64},{40,72},{48,80},{56,88},{64,... | collective-permute-start | bytes 835592 | tf_op jit(solution)/shard_map/ppermute | solution.py:12
  77.7 10.8 %collective-permute-start.5 = (f32[4,136,128]{2,1,0:T(8,128)S(1)}, f32[4,136,128]{2,1,0:T(8,128)S(1)}, u32[]{:S(2)}, u32[]{:S(2)}) collective-permute-start(f32[4,136,128]{2,1,0:T(8,128)S(1)} %pad_maximum_fusion.9), channel_id=1, source_target_pairs={{0,64},{8,72},{16,80},{24,88},{32,96},{40,104},{48,112},{56,120},{... | collective-permute-start | bytes 835592 | tf_op jit(solution)/shard_map/ppermute | solution.py:12
  84.2 35.0 %copy-start.18 = (pred[512,512]{1,0:T(8,128)(4,1)}, pred[512,512]{1,0:T(8,128)(4,1)S(1)}, u32[]{:S(2)}) copy-start(pred[512,512]{1,0:T(8,128)(4,1)S(1)} %iota_compare_fusion.4) | copy-start | bytes 786436
  88.5 30.0 %collective-permute-start.6 = (f32[4,136,128]{2,1,0:T(8,128)S(1)}, f32[4,136,128]{2,1,0:T(8,128)S(1)}, u32[]{:S(2)}, u32[]{:S(2)}) collective-permute-start(f32[4,136,128]{2,1,0:T(8,128)S(1)} %pad_maximum_fusion.10), channel_id=1, source_target_pairs={{0,128},{8,136},{16,144},{24,152},{32,160},{40,168},{48,176},{56,1... | collective-permute-start | bytes 835592 | tf_op jit(solution)/shard_map/ppermute | solution.py:12
  122.8 70.3 %copy-start.2 = (f32[4,512,128]{1,2,0:T(8,128)}, f32[4,512,128]{1,2,0:T(8,128)S(1)}, u32[]{:S(2)}) copy-start(f32[4,512,128]{1,2,0:T(8,128)S(1)} %get-tuple-element.57) | copy-start | bytes 3145732
  158.4 34.7 %copy-start.5 = (bf16[512,512]{0,1:T(8,128)(2,1)}, bf16[512,512]{0,1:T(8,128)(2,1)S(1)}, u32[]{:S(2)}) copy-start(bf16[512,512]{0,1:T(8,128)(2,1)S(1)} %convolution_convert_fusion.4) | copy-start | bytes 1572868
  160.4 10.9 %collective-permute-start.7 = (f32[4,136,128]{2,1,0:T(8,128)S(1)}, f32[4,136,128]{2,1,0:T(8,128)S(1)}, u32[]{:S(2)}, u32[]{:S(2)}) collective-permute-start(f32[4,136,128]{2,1,0:T(8,128)S(1)} %pad_maximum_fusion.3), channel_id=1, source_target_pairs={{8,0},{16,8},{24,16},{32,24},{40,32},{48,40},{56,48},{64,56},{72,6... | collective-permute-start | bytes 835592 | tf_op jit(solution)/shard_map/ppermute | solution.py:12
  171.2 8.5 %collective-permute-start.8 = (f32[4,136,128]{2,1,0:T(8,128)S(1)}, f32[4,136,128]{2,1,0:T(8,128)}, u32[]{:S(2)}, u32[]{:S(2)}) collective-permute-start(f32[4,136,128]{2,1,0:T(8,128)S(1)} %collective-permute-done.7), channel_id=1, source_target_pairs={{8,0},{16,8},{24,16},{32,24},{40,32},{48,40},{56,48},{64,56},{72,6... | collective-permute-start | bytes 835592 | tf_op jit(solution)/shard_map/ppermute | solution.py:12
  177.2 600.6 %all-gather.10.cloned.1.call-start = ((), (), s32[]{:S(2)}) async-start(), calls=%async_computation.5 | async-start | bytes 69746688 | tf_op jit(solution)/shard_map/all_gather | solution.py:202
  181.6 9.9 %collective-permute-start.9 = (f32[4,136,128]{2,1,0:T(8,128)S(1)}, f32[4,136,128]{2,1,0:T(8,128)S(1)}, u32[]{:S(2)}, u32[]{:S(2)}) collective-permute-start(f32[4,136,128]{2,1,0:T(8,128)S(1)} %pad_maximum_fusion.11), channel_id=1, source_target_pairs={{16,0},{24,8},{32,16},{40,24},{48,32},{56,40},{64,48},{72,56},{80,... | collective-permute-start | bytes 835592 | tf_op jit(solution)/shard_map/ppermute | solution.py:12
  191.6 9.8 %collective-permute-start.10 = (f32[4,136,128]{2,1,0:T(8,128)S(1)}, f32[4,136,128]{2,1,0:T(8,128)S(1)}, u32[]{:S(2)}, u32[]{:S(2)}) collective-permute-start(f32[4,136,128]{2,1,0:T(8,128)S(1)} %pad_maximum_fusion.12), channel_id=1, source_target_pairs={{32,0},{40,8},{48,16},{56,24},{64,32},{72,40},{80,48},{88,56},{96,... | collective-permute-start | bytes 835592 | tf_op jit(solution)/shard_map/ppermute | solution.py:12
  201.5 14.7 %collective-permute-start.11 = (f32[4,136,128]{2,1,0:T(8,128)S(1)}, f32[4,136,128]{2,1,0:T(8,128)S(1)}, u32[]{:S(2)}, u32[]{:S(2)}) collective-permute-start(f32[4,136,128]{2,1,0:T(8,128)S(1)} %pad_maximum_fusion.13), channel_id=1, source_target_pairs={{64,0},{72,8},{80,16},{88,24},{96,32},{104,40},{112,48},{120,56},{... | collective-permute-start | bytes 835592 | tf_op jit(solution)/shard_map/ppermute | solution.py:12
  216.3 15.1 %collective-permute-start.12 = (f32[4,136,128]{2,1,0:T(8,128)S(1)}, f32[4,136,128]{2,1,0:T(8,128)S(1)}, u32[]{:S(2)}, u32[]{:S(2)}) collective-permute-start(f32[4,136,128]{2,1,0:T(8,128)S(1)} %pad_maximum_fusion.14), channel_id=1, source_target_pairs={{128,0},{136,8},{144,16},{152,24},{160,32},{168,40},{176,48},{184,... | collective-permute-start | bytes 835592 | tf_op jit(solution)/shard_map/ppermute | solution.py:12
  237.7 6.5 collective-permute-start.13
  267.6 16.9 %copy-start.4 = (bf16[3,512,512]{1,2,0:T(8,128)(2,1)S(1)}, bf16[3,512,512]{1,2,0:T(8,128)(2,1)}, u32[]{:S(2)}) copy-start(bf16[3,512,512]{1,2,0:T(8,128)(2,1)} %get-tuple-element.60) | copy-start | bytes 4718596
  267.6 140.8 %all-to-all-start = ((bf16[32,512,128]{2,1,0:T(8,128)(2,1)}), bf16[32,512,128]{2,1,0:T(8,128)(2,1)}, u32[]{:S(2)}, u32[]{:S(2)}) async-start(bf16[32,512,128]{2,1,0:T(8,128)(2,1)} %bitcast.223), calls=%async_computation.1 | async-start | bytes 8388608 | tf_op jit(solution)/shard_map/all_to_all | solution.py:203
  (21 other events, 127.6 us)
Sparse Core Ops, SparseCore 0:
  9.8 36.5 all-gather.5
  48.9 103.5 all-gather.7
  177.3 35.1 reduce-scatter.1
  267.7 510.0 all-gather.9
